TPU v7x, 32 devices: a whole 2x2x4 slice. The times are simulated.
32 devices in a mesh: parts: 2 (over y), sub: 4 (over z), row: 2 (over x), col: 2 (over core).
Axes of the slice: x: 2, y: 2, z: 4, core: 2. Of those that a mesh axis runs over, the one named last changes fastest.
Arguments:
- loads: float32 [8, 32, 1024], P(('parts', 'sub'), 'col'), parts along dimension 0, may hold values from -6 to 6
- weights: float32 [8, 1024], P(('parts', 'sub')), parts along dimension 0, may hold values from 0.25 to 4
- dual_ops: bfloat16 [8, 2048, 2048], P(('parts', 'sub'), 'row'), parts along dimension 0, as said below
- corner_maps: bfloat16 [8, 24, 2048], P(('parts', 'sub'), None, 'row'), parts along dimension 0, may hold values from -0.25 to 0.25
- coarse_inverse: float32 [96, 48], P('parts'), parts along dimension 0, as said below
- corner_ids: int32 [8, 24], P('parts'), parts along dimension 0, may hold values from 0 to 47, as said below
- iface_sizes: int32 [8], P('parts'), parts along dimension 0, may hold values from 512 to 1024, as said below
- left_partner: int32 [8, 1024], P(('parts', 'sub')), parts along dimension 0, may hold values from 0 to 1023, as said below
- right_partner: int32 [8, 1024], P(('parts', 'sub')), parts along dimension 0, may hold values from 0 to 1023, as said below
Outputs:
- solution: float32 [8, 32, 1024], P(('parts', 'sub'), 'col'), parts along dimension 0
- residual: float32 [8, 32, 1024], P(('parts', 'sub'), 'col'), parts along dimension 0
There are 2 independent parts, one for each index of `parts`. A program takes and returns all parts, laid end to end along the dimension named above; each array names one. Nothing has to cross between parts.
Inputs may be any that keep to these rules, and one draw needn't show every extreme that they name: Global indices 24/2 * s to 24/2 * s + 24/2 - 1 are the corners of the interface between s and s+1; the first half of subdomain s's corner_ids is a permutation of those of interface s-1, the second half a permutation of those of interface s. `left_partner`: each row s is a permutation that maps the slots below iface_sizes[s-1] onto slots below it. `right_partner`: each row s is a permutation that maps the slots below iface_sizes[s] onto slots below it, and is the inverse of left_partner[s+1]. `dual_ops`: symmetric positive definite. `coarse_inverse`: symmetric positive definite. For each s < 2, one of iface_sizes[s] and iface_sizes[s + 2] is 896 or more and the other 640 or less.
All inputs are finite; a program needn't handle non-finite values.
Results may differ from a plain program's by a relative error of at most 0.015.
Values may be sent and summed in bfloat16 or wider, within the bound.
No kernel may reach another device: no remote copies, remote signals or barrier semaphores. Data moves between devices by JAX's collectives and lax.ppermute only.
A program may use at most 64 MiB of HBM per device.

v0:
```python
import jax
import jax.numpy as jnp
from jax import lax
from jax.sharding import PartitionSpec as P

TILE = 128
ITERS = 2


def shifted(value, axis, steps):
    count = lax.axis_size(axis)
    pairs = [(source, (source + steps) % count) for source in range(count)]
    return lax.ppermute(value, axis, pairs)


def inner(first, second, half):
    return jnp.sum(first[:, :half] * second[:, :half], axis=1)


def paired_totals(residual, precond, image, half):
    return lax.psum((inner(residual, precond, half), inner(precond, image, half)), "sub")


def tile_products(vector, rows_op, first_tile, last_tile, output):

    def one_tile(tile_at, acc):
        piece = lax.dynamic_slice_in_dim(rows_op, tile_at * TILE, TILE, 0)
        product = lax.dot_general(
            vector, piece, (((1,), (1,)), ((), ())), preferred_element_type=jnp.float32
        )
        return lax.dynamic_update_slice_in_dim(acc, product, tile_at * TILE, 1)

    return lax.fori_loop(first_tile, last_tile, one_tile, output)


def live_tiles(size_before, size_after, block_start, block, half):
    left_live = jnp.clip(size_before - block_start, 0, block)
    right_live = jnp.clip(size_after - (block_start - half), 0, block)
    live_cols = jnp.where(block_start < half, left_live, right_live)
    return (live_cols + TILE - 1) // TILE


def per_device(
    loads,
    weights,
    dual_ops,
    corner_maps,
    coarse_inverse,
    corner_ids,
    iface_sizes,
    left_partner,
    right_partner,
):
    half = loads.shape[2]
    block = dual_ops.shape[1]
    width = coarse_inverse.shape[0]
    subdomain = lax.axis_index("sub")
    count = lax.axis_size("sub")
    row_index = lax.axis_index("row")
    left_map = left_partner[0]
    right_map = right_partner[0]
    slots = jnp.arange(half, dtype=jnp.int32)
    size_before = iface_sizes[(subdomain + count - 1) % count]
    size_after = iface_sizes[subdomain]
    live_left = (slots < size_before).astype(jnp.float32)
    live_right = (right_map < size_after).astype(jnp.float32)
    columns = jnp.arange(width, dtype=jnp.int32)
    own_hot = (corner_ids[subdomain][:, None] == columns[None, :]).astype(jnp.float32)
    operator = dual_ops[0]
    coupling = corner_maps[0]
    block_start = row_index * block
    own_tiles = live_tiles(size_before, size_after, block_start, block, half)

    def apply_operator(vec):
        halfway = vec.astype(jnp.bfloat16)
        empty = jnp.zeros((halfway.shape[0], block), jnp.float32)
        local = tile_products(halfway, operator, jnp.int32(0), own_tiles, empty)
        own_slots = lax.dynamic_slice_in_dim(halfway, row_index * block, block, 1)
        corner = lax.dot_general(
            own_slots, coupling, (((1,), (1,)), ((), ())), preferred_element_type=jnp.float32
        )
        scattered = jnp.dot(corner, own_hot, precision=lax.Precision.HIGHEST)
        coarse = lax.psum(scattered, ("sub", "row"))
        solved = jnp.dot(coarse, coarse_inverse, precision=lax.Precision.HIGHEST)
        back = lax.dot_general(
            solved, own_hot, (((1,), (1,)), ((), ())), precision=lax.Precision.HIGHEST
        ).astype(jnp.bfloat16)
        united = local + jnp.dot(back, coupling, preferred_element_type=jnp.float32)
        whole = lax.all_gather(united.astype(jnp.bfloat16), "row", axis=1, tiled=True).astype(
            united.dtype
        )
        lower = whole[:, :half]
        upper = whole[:, half:]
        arrived_left = shifted(upper.astype(jnp.bfloat16), "sub", 1).astype(upper.dtype)
        arrived_right = shifted(lower.astype(jnp.bfloat16), "sub", -1).astype(lower.dtype)
        result_left = (lower + jnp.take(arrived_left, left_map, axis=1)) * live_left
        result_right = (upper + jnp.take(arrived_right, right_map, axis=1)) * live_right
        return jnp.concatenate([result_left, result_right], axis=1)

    received = (
        shifted(loads[0].astype(jnp.bfloat16), "sub", -1).astype(jnp.float32),
        shifted(weights.astype(jnp.bfloat16), "sub", -1).astype(weights.dtype),
    )
    right_load = jnp.take(received[0], right_map, axis=1) * live_right
    right_weight = jnp.take(received[1], right_map, axis=1)
    residual = jnp.concatenate([loads[0] * live_left, right_load], axis=1)
    scaling = jnp.concatenate([weights, right_weight], axis=1)
    solution = jnp.zeros_like(residual)
    precond = scaling * residual
    image = apply_operator(precond)
    gamma, delta = paired_totals(residual, precond, image, half)
    alpha = gamma / delta
    direction = precond
    along = image
    for step in range(ITERS):
        solution = solution + alpha[:, None] * direction
        residual = residual - alpha[:, None] * along
        if step + 1 < ITERS:
            precond = scaling * residual
            image = apply_operator(precond)
            gamma_next, delta = paired_totals(residual, precond, image, half)
            ratio = gamma_next / gamma
            alpha = gamma_next / (delta - ratio * gamma_next / alpha)
            direction = precond + ratio[:, None] * direction
            along = image + ratio[:, None] * along
            gamma = gamma_next
    return (solution[:, :half][None], residual[:, :half][None])


def solution(mesh):
    placed = (
        P(("parts", "sub"), "col", None),
        P(("parts", "sub"), None),
        P(("parts", "sub"), "row", None),
        P(("parts", "sub"), None, "row"),
        P("parts", None),
        P("parts", None),
        P("parts"),
        P(("parts", "sub"), None),
        P(("parts", "sub"), None),
    )
    return jax.shard_map(
        per_device,
        mesh=mesh,
        in_specs=placed,
        out_specs=(P(("parts", "sub"), "col", None), P(("parts", "sub"), "col", None)),
        check_vma=False,
    )
```

profile of v0, /device:TPU:0, one launch (start us, length us, event | category | flops | bytes accessed | tf_op | source)
XLA Modules:
  0.0 136.2 jit_solution(17909804324471528583)
XLA Ops:
  1.5 5.1 %collective-permute-start.1 = (bf16[16,1024]{1,0:T(8,128)(2,1)S(1)}, bf16[16,1024]{1,0:T(8,128)(2,1)S(1)}, u32[]{:S(2)}, u32[]{:S(2)}) collective-permute-start(bf16[16,1024]{1,0:T(8,128)(2,1)S(1)} %bitcast_convert_fusion), channel_id=1, source_target_pairs={{0,12},{4,0},{8,4},{12,8},{1,13},{5,1},{9,5},{13,9},{2,14},{6,2},{... | collective-permute-start | bytes 98312 | tf_op jit(solution)/shard_map/ppermute | solution.py:13
  9.1 1.3 fusion.49
  10.5 1.3 fusion.35
  11.8 1.3 compare_convert_fusion
  16.7 4.5 %gather_fusion = f32[1024]{0:T(1024)S(1)} fusion(f32[1024]{0:T(1024)S(1)} %bitcast.80, s32[1024]{0:T(1024)S(1)} %broadcast_clamp_fusion), kind=kCustom, calls=%fused_computation.5 | custom fusion | bytes 12288 | tf_op jit(solution)/shard_map/jit(_take)/gather | solution.py:105
  21.5 2.8 %gather_fusion.1 = f32[1024,16]{1,0:T(8,128)S(1)} fusion(f32[16,1024]{0,1:T(8,128)S(1)} %copy.21, s32[1024]{0:T(1024)S(1)} %fusion.36), kind=kCustom, calls=%fused_computation.clone | custom fusion | bytes 135168 | tf_op jit(solution)/shard_map/jit(_take)/gather | solution.py:104
  24.5 10.4 %while.20 = (s32[]{:T(128)}, f32[16,1024]{1,0:T(8,128)S(1)}, s32[]{:T(128)}, bf16[1024,2048]{1,0:T(8,128)(2,1)}, bf16[16,2048]{1,0:T(8,128)(2,1)S(1)}, /*index=5*/s32[]{:T(128)}, s32[]{:T(128)}, s32[]{:T(128)}, s32[]{:T(128)}) while((s32[]{:T(128)}, f32[16,1024]{1,0:T(8,128)S(1)}, s32[]{:T(128)}, bf16[1024,2048]{1,0:T(8,128)(2,1)}, ...), condition=%wide.region_3.5_spmd, body=%wide.region_2.4_spmd.sunk | while | flops 8388614 | bytes 599179 | solution.py:33
  25.9 1.3 fusion.72
  27.1 1.3 fusion.72
  35.3 18.9 %psum.43 = f32[16,48]{1,0:T(8,128)S(1)} all-reduce(f32[16,48]{1,0:T(8,128)S(1)} %fusion.30), channel_id=1, replica_groups=mesh['parts'=2,'sub'=4,'row'=2,'col'=2] {'sub','row'}, use_global_device_ids=true, to_apply=%region_4.6 | all-reduce | flops 768 | bytes 6144 | tf_op jit(solution)/shard_map/psum | solution.py:83
  54.6 4.6 %all_gather.6 = bf16[16,2048]{1,0:T(8,128)(2,1)S(1)} all-gather(bf16[16,1024]{1,0:T(8,128)(2,1)S(1)} %fusion.6), channel_id=1, replica_groups=mesh['parts'=2,'sub'=4,'row'=2,'col'=2] {'row'}, dimensions={1}, use_global_device_ids=true | all-gather | bytes 98304 | tf_op jit(solution)/shard_map/all_gather | solution.py:89
  59.2 3.8 %collective-permute-start.3 = (bf16[16,1024]{1,0:T(8,128)(2,1)S(1)}, bf16[16,1024]{1,0:T(8,128)(2,1)S(1)}, u32[]{:S(2)}, u32[]{:S(2)}) collective-permute-start(bf16[16,1024]{1,0:T(8,128)(2,1)S(1)} %get-tuple-element.103), channel_id=1, source_target_pairs={{0,12},{4,0},{8,4},{12,8},{1,13},{5,1},{9,5},{13,9},{2,14},{6,2},{... | collective-permute-start | bytes 98312 | tf_op jit(solution)/shard_map/ppermute | solution.py:13
  63.1 1.9 %collective-permute-done.2 = bf16[16,1024]{1,0:T(8,128)(2,1)S(1)} collective-permute-done((bf16[16,1024]{1,0:T(8,128)(2,1)S(1)}, bf16[16,1024]{1,0:T(8,128)(2,1)S(1)}, u32[]{:S(2)}, u32[]{:S(2)}) %collective-permute-start.2) | collective-permute-done | bytes 32800 | tf_op jit(solution)/shard_map/ppermute | solution.py:13
  65.1 2.8 %gather_fusion.2 = f32[1024,16]{1,0:T(8,128)S(1)} fusion(f32[16,1024]{0,1:T(8,128)S(1)} %copy.23, s32[1024]{0:T(1024)S(1)} %fusion.37), kind=kCustom, calls=%fused_computation.1.clone | custom fusion | bytes 135168 | tf_op jit(solution)/shard_map/jit(_take)/gather | solution.py:96
  68.2 2.8 %gather_fusion.3 = f32[1024,16]{1,0:T(8,128)S(1)} fusion(f32[16,1024]{0,1:T(8,128)S(1)} %copy.25, s32[1024]{0:T(1024)S(1)} %fusion.36), kind=kCustom, calls=%fused_computation.2.clone | custom fusion | bytes 135168 | tf_op jit(solution)/shard_map/jit(_take)/gather | solution.py:97
  71.3 9.1 %all-reduce.1 = (f32[16]{0:T(128)S(1)}, f32[16]{0:T(128)S(1)}) all-reduce(f32[16]{0:T(128)S(1)} %get-tuple-element.64, f32[16]{0:T(128)S(1)} %get-tuple-element.63), channel_id=1, replica_groups=mesh['parts'=2,'sub'=4,'row'=2,'col'=2] {'sub'}, use_global_device_ids=true, to_apply=%region_1.3 | all-reduce | flops 32 | bytes 256 | tf_op jit(solution)/shard_map/psum | solution.py:21
  80.6 10.3 %while.21 = (s32[]{:T(128)}, f32[16,1024]{1,0:T(8,128)S(1)}, s32[]{:T(128)}, bf16[1024,2048]{1,0:T(8,128)(2,1)}, bf16[16,2048]{1,0:T(8,128)(2,1)S(1)}, /*index=5*/s32[]{:T(128)}, s32[]{:T(128)}, s32[]{:T(128)}, s32[]{:T(128)}) while((s32[]{:T(128)}, f32[16,1024]{1,0:T(8,128)S(1)}, s32[]{:T(128)}, bf16[1024,2048]{1,0:T(8,128)(2,1)}, ...), condition=%wide.region_10.12_spmd, body=%wide.region_9.11_spmd.sunk | while | flops 8388614 | bytes 599179 | solution.py:33
  91.2 18.7 %psum.46 = f32[16,48]{1,0:T(8,128)S(1)} all-reduce(f32[16,48]{1,0:T(8,128)S(1)} %fusion.29), channel_id=1, replica_groups=mesh['parts'=2,'sub'=4,'row'=2,'col'=2] {'sub','row'}, use_global_device_ids=true, to_apply=%region_11.13 | all-reduce | flops 768 | bytes 6144 | tf_op jit(solution)/shard_map/psum | solution.py:83
  110.3 4.6 %all_gather.7 = bf16[16,2048]{1,0:T(8,128)(2,1)S(1)} all-gather(bf16[16,1024]{1,0:T(8,128)(2,1)S(1)} %fusion.7), channel_id=1, replica_groups=mesh['parts'=2,'sub'=4,'row'=2,'col'=2] {'row'}, dimensions={1}, use_global_device_ids=true | all-gather | bytes 98304 | tf_op jit(solution)/shard_map/all_gather | solution.py:89
  114.9 2.0 %collective-permute-start.4 = (bf16[16,1024]{1,0:T(8,128)(2,1)S(1)}, bf16[16,1024]{1,0:T(8,128)(2,1)S(1)}, u32[]{:S(2)}, u32[]{:S(2)}) collective-permute-start(bf16[16,1024]{1,0:T(8,128)(2,1)S(1)} %get-tuple-element.101), channel_id=1, source_target_pairs={{0,4},{4,8},{8,12},{12,0},{1,5},{5,9},{9,13},{13,1},{2,6},{6,10},{... | collective-permute-start | bytes 98312 | tf_op jit(solution)/shard_map/ppermute | solution.py:13
  117.0 1.9 %collective-permute-done.5 = bf16[16,1024]{1,0:T(8,128)(2,1)S(1)} collective-permute-done((bf16[16,1024]{1,0:T(8,128)(2,1)S(1)}, bf16[16,1024]{1,0:T(8,128)(2,1)S(1)}, u32[]{:S(2)}, u32[]{:S(2)}) %collective-permute-start.5) | collective-permute-done | bytes 32800 | tf_op jit(solution)/shard_map/ppermute | solution.py:13
  119.0 2.8 %gather_fusion.5 = f32[1024,16]{1,0:T(8,128)S(1)} fusion(f32[16,1024]{0,1:T(8,128)S(1)} %copy.29, s32[1024]{0:T(1024)S(1)} %fusion.36), kind=kCustom, calls=%fused_computation.4.clone | custom fusion | bytes 135168 | tf_op jit(solution)/shard_map/jit(_take)/gather | solution.py:97
  122.1 2.8 %gather_fusion.4 = f32[1024,16]{1,0:T(8,128)S(1)} fusion(f32[16,1024]{0,1:T(8,128)S(1)} %copy.27, s32[1024]{0:T(1024)S(1)} %fusion.37), kind=kCustom, calls=%fused_computation.3.clone | custom fusion | bytes 135168 | tf_op jit(solution)/shard_map/jit(_take)/gather | solution.py:96
  125.3 10.2 %all-reduce = (f32[16]{0:T(128)S(1)}, f32[16]{0:T(128)S(1)}) all-reduce(f32[16]{0:T(128)S(1)} %get-tuple-element.62, f32[16]{0:T(128)S(1)} %get-tuple-element.61), channel_id=1, replica_groups=mesh['parts'=2,'sub'=4,'row'=2,'col'=2] {'sub'}, use_global_device_ids=true, to_apply=%region_8.10 | all-reduce | flops 32 | bytes 256 | tf_op jit(solution)/shard_map/psum | solution.py:21
  (79 shorter events, 28.2 us)
Async XLA Ops:
  0.6 34.3 %copy-start = (bf16[1,24,1024]{2,1,0:T(8,128)(2,1)S(1)}, bf16[1,24,1024]{2,1,0:T(8,128)(2,1)}, u32[]{:S(2)}) copy-start(bf16[1,24,1024]{2,1,0:T(8,128)(2,1)} %param.18) | copy-start | bytes 147460
  0.6 20.7 %copy-start.5 = (f32[1,1024]{1,0:T(1,128)S(1)}, f32[1,1024]{1,0:T(1,128)}, u32[]{:S(2)}) copy-start(f32[1,1024]{1,0:T(1,128)} %param.16) | copy-start | bytes 12292
  0.7 20.6 %copy-start.2 = (s32[1,1024]{1,0:T(1,128)S(1)}, s32[1,1024]{1,0:T(1,128)}, u32[]{:S(2)}) copy-start(s32[1,1024]{1,0:T(1,128)} %param.23) | copy-start | bytes 12292
  1.5 19.8 %collective-permute-start.1 = (bf16[16,1024]{1,0:T(8,128)(2,1)S(1)}, bf16[16,1024]{1,0:T(8,128)(2,1)S(1)}, u32[]{:S(2)}, u32[]{:S(2)}) collective-permute-start(bf16[16,1024]{1,0:T(8,128)(2,1)S(1)} %bitcast_convert_fusion), channel_id=1, source_target_pairs={{0,12},{4,0},{8,4},{12,8},{1,13},{5,1},{9,5},{13,9},{2,14},{6,2},{... | collective-permute-start | bytes 98312 | tf_op jit(solution)/shard_map/ppermute | solution.py:13
  7.3 9.4 %collective-permute-start = (bf16[1,1024]{1,0:T(2,128)(2,1)S(1)}, bf16[1,1024]{1,0:T(2,128)(2,1)S(1)}, u32[]{:S(2)}, u32[]{:S(2)}) collective-permute-start(bf16[1,1024]{1,0:T(2,128)(2,1)S(1)} %convert_element_type.71), channel_id=1, source_target_pairs={{0,12},{4,0},{8,4},{12,8},{1,13},{5,1},{9,5},{13,9},{2,14},{6,2},{... | collective-permute-start | bytes 6152 | tf_op jit(solution)/shard_map/ppermute | solution.py:13
  16.7 37.4 %copy-start.3 = (f32[48,48]{1,0:T(8,128)S(1)}, f32[48,48]{1,0:T(8,128)}, u32[]{:S(2)}) copy-start(f32[48,48]{1,0:T(8,128)} %param.19) | copy-start | bytes 27652
  16.7 46.3 %copy-start.4 = (s32[1,1024]{1,0:T(1,128)S(1)}, s32[1,1024]{1,0:T(1,128)}, u32[]{:S(2)}) copy-start(s32[1,1024]{1,0:T(1,128)} %param.22) | copy-start | bytes 12292
  24.5 46.7 %copy-start.1 = (f32[1,16,1024]{2,1,0:T(8,128)S(1)}, f32[1,16,1024]{2,1,0:T(8,128)}, u32[]{:S(2)}) copy-start(f32[1,16,1024]{2,1,0:T(8,128)} %param.15) | copy-start | bytes 196612
  59.2 5.7 %collective-permute-start.2 = (bf16[16,1024]{1,0:T(8,128)(2,1)S(1)}, bf16[16,1024]{1,0:T(8,128)(2,1)S(1)}, u32[]{:S(2)}, u32[]{:S(2)}) collective-permute-start(bf16[16,1024]{1,0:T(8,128)(2,1)S(1)} %get-tuple-element.102), channel_id=1, source_target_pairs={{0,4},{4,8},{8,12},{12,0},{1,5},{5,9},{9,13},{13,1},{2,6},{6,10},{... | collective-permute-start | bytes 98312 | tf_op jit(solution)/shard_map/ppermute | solution.py:13
  59.2 8.8 %collective-permute-start.3 = (bf16[16,1024]{1,0:T(8,128)(2,1)S(1)}, bf16[16,1024]{1,0:T(8,128)(2,1)S(1)}, u32[]{:S(2)}, u32[]{:S(2)}) collective-permute-start(bf16[16,1024]{1,0:T(8,128)(2,1)S(1)} %get-tuple-element.103), channel_id=1, source_target_pairs={{0,12},{4,0},{8,4},{12,8},{1,13},{5,1},{9,5},{13,9},{2,14},{6,2},{... | collective-permute-start | bytes 98312 | tf_op jit(solution)/shard_map/ppermute | solution.py:13
  114.9 3.9 %collective-permute-start.5 = (bf16[16,1024]{1,0:T(8,128)(2,1)S(1)}, bf16[16,1024]{1,0:T(8,128)(2,1)S(1)}, u32[]{:S(2)}, u32[]{:S(2)}) collective-permute-start(bf16[16,1024]{1,0:T(8,128)(2,1)S(1)} %get-tuple-element.100), channel_id=1, source_target_pairs={{0,12},{4,0},{8,4},{12,8},{1,13},{5,1},{9,5},{13,9},{2,14},{6,2},{... | collective-permute-start | bytes 98312 | tf_op jit(solution)/shard_map/ppermute | solution.py:13
  114.9 7.0 %collective-permute-start.4 = (bf16[16,1024]{1,0:T(8,128)(2,1)S(1)}, bf16[16,1024]{1,0:T(8,128)(2,1)S(1)}, u32[]{:S(2)}, u32[]{:S(2)}) collective-permute-start(bf16[16,1024]{1,0:T(8,128)(2,1)S(1)} %get-tuple-element.101), channel_id=1, source_target_pairs={{0,4},{4,8},{8,12},{12,0},{1,5},{5,9},{9,13},{13,1},{2,6},{6,10},{... | collective-permute-start | bytes 98312 | tf_op jit(solution)/shard_map/ppermute | solution.py:13
where the time goes:
time: 137 us; the launch traced here: 136 us
  blocking collectives  65.9 us (48%)
  matrix products  22.3 us (16%)
  local copies, waits for them, and re-layouts  22.1 us (16%)
  starting transfers between devices  11.4 us (8%)
  other arithmetic  8.41 us (6%)
  waiting for transfers between devices  3.74 us (3%)
  between operations  2.25 us (2%)
    psum x2, blocking collectives, apply_operator(): coarse = lax.psum(scattered, ('sub', 'row'))  37.5 us
    dot_general x16, matrix products, one_tile(): lax.dot_general(vector, piece, (((1,), (1,)), ((), ())), preferred_elemen...  20.7 us
    psum x2, blocking collectives, paired_totals(): lax.psum((inner(residual, precond, half), inner(precond, image, half)), '...  19.2 us
    ppermute x6, starting transfers between devices, shifted(): return lax.ppermute(value, axis, pairs)  11.4 us
    all_gather x2, blocking collectives, apply_operator(): lax.all_gather(united.astype(jnp.bfloat16), 'row', axis=1, tiled=True)  9.15 us
    gather x4, local copies, waits for them, and re-layouts, apply_operator(): jnp.take(arrived_right, right_map, axis=1)  5.95 us
    gather x4, local copies, waits for them, and re-layouts, apply_operator(): result_left = (lower + jnp.take(arrived_left, left_map, axis=1)) * live_left  5.95 us
    gather x1, local copies, waits for them, and re-layouts, per_device(): right_weight = jnp.take(received[1], right_map, axis=1)  4.53 us
  transfers between devices with their start and end apart: 6, of which 2 were waited for; matrix products, arithmetic and copies ran while one was open for 14% of the time, Pallas kernels for 0%

commit v1 on v0

--- a/solution.py
+++ b/solution.py
@@ -5,6 +5,12 @@
 
 TILE = 128
 ITERS = 2
+
+
+def finish_the_panels(local_block):
+    d_next = lax.all_gather(local_block, ("sub", "row"))
+    w1 = jnp.sum(d_next, 0)
+    return w1
 
 
 def shifted(value, axis, steps):
@@ -80,7 +86,7 @@
             own_slots, coupling, (((1,), (1,)), ((), ())), preferred_element_type=jnp.float32
         )
         scattered = jnp.dot(corner, own_hot, precision=lax.Precision.HIGHEST)
-        coarse = lax.psum(scattered, ("sub", "row"))
+        coarse = finish_the_panels(scattered)
         solved = jnp.dot(coarse, coarse_inverse, precision=lax.Precision.HIGHEST)
         back = lax.dot_general(
             solved, own_hot, (((1,), (1,)), ((), ())), precision=lax.Precision.HIGHEST

time: 137 us -> 162 us (1.18)
  blocking collectives: 65.9 us -> 90.2 us
    all_gather x0 -> x2, blocking collectives: none -> 61.2 us  [finish_the_panels(): d_next = lax.all_gather(local_block, ('sub', 'row'))]
    psum x2 -> x0, blocking collectives: 37.5 us -> none  [apply_operator(): coarse = lax.psum(scattered, ('sub', 'row'))]
  transfers between devices with their start and end apart: 6 -> 6, of which waited for: 2 -> 2; matrix products, arithmetic and copies ran while one was open for 14% -> 12% of each run, Pallas kernels for 0% -> 0%
where the time goes in v1:
time: 162 us; the launch traced here: 160 us
  blocking collectives  90.2 us (56%)
  matrix products  22.3 us (14%)
  local copies, waits for them, and re-layouts  22.1 us (14%)
  starting transfers between devices  11.4 us (7%)
  other arithmetic  8.44 us (5%)
  waiting for transfers between devices  3.76 us (2%)
  between operations  2.23 us (1%)
    all_gather x2, blocking collectives, finish_the_panels(): d_next = lax.all_gather(local_block, ('sub', 'row'))  61.2 us
    dot_general x16, matrix products, one_tile(): lax.dot_general(vector, piece, (((1,), (1,)), ((), ())), preferred_elemen...  20.7 us
    psum x2, blocking collectives, paired_totals(): lax.psum((inner(residual, precond, half), inner(precond, image, half)), '...  19.8 us
    ppermute x6, starting transfers between devices, shifted(): return lax.ppermute(value, axis, pairs)  11.4 us
    all_gather x2, blocking collectives, apply_operator(): lax.all_gather(united.astype(jnp.bfloat16), 'row', axis=1, tiled=True)  9.15 us
    gather x4, local copies, waits for them, and re-layouts, apply_operator(): jnp.take(arrived_right, right_map, axis=1)  5.95 us
    gather x4, local copies, waits for them, and re-layouts, apply_operator(): result_left = (lower + jnp.take(arrived_left, left_map, axis=1)) * live_left  5.95 us
    gather x1, local copies, waits for them, and re-layouts, per_device(): right_weight = jnp.take(received[1], right_map, axis=1)  4.53 us
  transfers between devices with their start and end apart: 6, of which 2 were waited for; matrix products, arithmetic and copies ran while one was open for 12% of the time, Pallas kernels for 0%

profile of v1, /device:TPU:0, one launch (start us, length us, event | category | flops | bytes accessed | tf_op | source)
XLA Modules:
  0.0 160.5 jit_solution(12804455485948178169)
XLA Ops:
  1.5 5.1 %collective-permute-start.1 = (bf16[16,1024]{1,0:T(8,128)(2,1)S(1)}, bf16[16,1024]{1,0:T(8,128)(2,1)S(1)}, u32[]{:S(2)}, u32[]{:S(2)}) collective-permute-start(bf16[16,1024]{1,0:T(8,128)(2,1)S(1)} %bitcast_convert_fusion), channel_id=1, source_target_pairs={{0,12},{4,0},{8,4},{12,8},{1,13},{5,1},{9,5},{13,9},{2,14},{6,2},{... | collective-permute-start | bytes 98312 | tf_op jit(solution)/shard_map/ppermute | solution.py:19
  9.1 1.3 fusion.49
  10.5 1.3 fusion.35
  11.8 1.3 compare_convert_fusion
  16.7 4.5 %gather_fusion = f32[1024]{0:T(1024)S(1)} fusion(f32[1024]{0:T(1024)S(1)} %bitcast.82, s32[1024]{0:T(1024)S(1)} %broadcast_clamp_fusion), kind=kCustom, calls=%fused_computation.5 | custom fusion | bytes 12288 | tf_op jit(solution)/shard_map/jit(_take)/gather | solution.py:111
  21.5 2.8 %gather_fusion.1 = f32[1024,16]{1,0:T(8,128)S(1)} fusion(f32[16,1024]{0,1:T(8,128)S(1)} %copy.21, s32[1024]{0:T(1024)S(1)} %fusion.36), kind=kCustom, calls=%fused_computation.clone | custom fusion | bytes 135168 | tf_op jit(solution)/shard_map/jit(_take)/gather | solution.py:110
  24.5 10.4 %while.20 = (s32[]{:T(128)}, f32[16,1024]{1,0:T(8,128)S(1)}, s32[]{:T(128)}, bf16[1024,2048]{1,0:T(8,128)(2,1)}, bf16[16,2048]{1,0:T(8,128)(2,1)S(1)}, /*index=5*/s32[]{:T(128)}, s32[]{:T(128)}, s32[]{:T(128)}, s32[]{:T(128)}) while((s32[]{:T(128)}, f32[16,1024]{1,0:T(8,128)S(1)}, s32[]{:T(128)}, bf16[1024,2048]{1,0:T(8,128)(2,1)}, ...), condition=%wide.region_3.5_spmd, body=%wide.region_2.4_spmd.sunk | while | flops 8388614 | bytes 599179 | solution.py:39
  25.9 1.3 fusion.72
  27.1 1.3 fusion.72
  35.3 30.6 %all-gather = f32[128,48]{1,0:T(8,128)S(1)} all-gather(f32[16,48]{1,0:T(8,128)S(1)} %fusion.30), channel_id=2, replica_groups=mesh['parts'=2,'sub'=4,'row'=2,'col'=2] {'sub','row'}, dimensions={0}, use_global_device_ids=true | all-gather | bytes 27648 | tf_op jit(solution)/shard_map/all_gather | solution.py:11
  66.4 4.6 %all_gather.20 = bf16[16,2048]{1,0:T(8,128)(2,1)S(1)} all-gather(bf16[16,1024]{1,0:T(8,128)(2,1)S(1)} %fusion.6), channel_id=1, replica_groups=mesh['parts'=2,'sub'=4,'row'=2,'col'=2] {'row'}, dimensions={1}, use_global_device_ids=true | all-gather | bytes 98304 | tf_op jit(solution)/shard_map/all_gather | solution.py:95
  71.0 3.8 %collective-permute-start.3 = (bf16[16,1024]{1,0:T(8,128)(2,1)S(1)}, bf16[16,1024]{1,0:T(8,128)(2,1)S(1)}, u32[]{:S(2)}, u32[]{:S(2)}) collective-permute-start(bf16[16,1024]{1,0:T(8,128)(2,1)S(1)} %get-tuple-element.103), channel_id=1, source_target_pairs={{0,12},{4,0},{8,4},{12,8},{1,13},{5,1},{9,5},{13,9},{2,14},{6,2},{... | collective-permute-start | bytes 98312 | tf_op jit(solution)/shard_map/ppermute | solution.py:19
  74.8 1.9 %collective-permute-done.2 = bf16[16,1024]{1,0:T(8,128)(2,1)S(1)} collective-permute-done((bf16[16,1024]{1,0:T(8,128)(2,1)S(1)}, bf16[16,1024]{1,0:T(8,128)(2,1)S(1)}, u32[]{:S(2)}, u32[]{:S(2)}) %collective-permute-start.2) | collective-permute-done | bytes 32800 | tf_op jit(solution)/shard_map/ppermute | solution.py:19
  76.8 2.8 %gather_fusion.2 = f32[1024,16]{1,0:T(8,128)S(1)} fusion(f32[16,1024]{0,1:T(8,128)S(1)} %copy.23, s32[1024]{0:T(1024)S(1)} %fusion.37), kind=kCustom, calls=%fused_computation.1.clone | custom fusion | bytes 135168 | tf_op jit(solution)/shard_map/jit(_take)/gather | solution.py:102
  80.0 2.8 %gather_fusion.3 = f32[1024,16]{1,0:T(8,128)S(1)} fusion(f32[16,1024]{0,1:T(8,128)S(1)} %copy.25, s32[1024]{0:T(1024)S(1)} %fusion.36), kind=kCustom, calls=%fused_computation.2.clone | custom fusion | bytes 135168 | tf_op jit(solution)/shard_map/jit(_take)/gather | solution.py:103
  83.1 9.0 %all-reduce.1 = (f32[16]{0:T(128)S(1)}, f32[16]{0:T(128)S(1)}) all-reduce(f32[16]{0:T(128)S(1)} %get-tuple-element.64, f32[16]{0:T(128)S(1)} %get-tuple-element.63), channel_id=1, replica_groups=mesh['parts'=2,'sub'=4,'row'=2,'col'=2] {'sub'}, use_global_device_ids=true, to_apply=%region_1.3 | all-reduce | flops 32 | bytes 256 | tf_op jit(solution)/shard_map/psum | solution.py:27
  92.4 10.3 %while.21 = (s32[]{:T(128)}, f32[16,1024]{1,0:T(8,128)S(1)}, s32[]{:T(128)}, bf16[1024,2048]{1,0:T(8,128)(2,1)}, bf16[16,2048]{1,0:T(8,128)(2,1)S(1)}, /*index=5*/s32[]{:T(128)}, s32[]{:T(128)}, s32[]{:T(128)}, s32[]{:T(128)}) while((s32[]{:T(128)}, f32[16,1024]{1,0:T(8,128)S(1)}, s32[]{:T(128)}, bf16[1024,2048]{1,0:T(8,128)(2,1)}, ...), condition=%wide.region_10.12_spmd, body=%wide.region_9.11_spmd.sunk | while | flops 8388614 | bytes 599179 | solution.py:39
  102.9 30.6 %all-gather.1 = f32[128,48]{1,0:T(8,128)S(1)} all-gather(f32[16,48]{1,0:T(8,128)S(1)} %fusion.29), channel_id=3, replica_groups=mesh['parts'=2,'sub'=4,'row'=2,'col'=2] {'sub','row'}, dimensions={0}, use_global_device_ids=true | all-gather | bytes 27648 | tf_op jit(solution)/shard_map/all_gather | solution.py:11
  134.0 4.6 %all_gather.23 = bf16[16,2048]{1,0:T(8,128)(2,1)S(1)} all-gather(bf16[16,1024]{1,0:T(8,128)(2,1)S(1)} %fusion.7), channel_id=1, replica_groups=mesh['parts'=2,'sub'=4,'row'=2,'col'=2] {'row'}, dimensions={1}, use_global_device_ids=true | all-gather | bytes 98304 | tf_op jit(solution)/shard_map/all_gather | solution.py:95
  139.2 1.5 collective-permute-start.4
  140.7 1.9 %collective-permute-done.5 = bf16[16,1024]{1,0:T(8,128)(2,1)S(1)} collective-permute-done((bf16[16,1024]{1,0:T(8,128)(2,1)S(1)}, bf16[16,1024]{1,0:T(8,128)(2,1)S(1)}, u32[]{:S(2)}, u32[]{:S(2)}) %collective-permute-start.5) | collective-permute-done | bytes 32800 | tf_op jit(solution)/shard_map/ppermute | solution.py:19
  142.7 2.8 %gather_fusion.5 = f32[1024,16]{1,0:T(8,128)S(1)} fusion(f32[16,1024]{0,1:T(8,128)S(1)} %copy.29, s32[1024]{0:T(1024)S(1)} %fusion.36), kind=kCustom, calls=%fused_computation.4.clone | custom fusion | bytes 135168 | tf_op jit(solution)/shard_map/jit(_take)/gather | solution.py:103
  145.8 2.8 %gather_fusion.4 = f32[1024,16]{1,0:T(8,128)S(1)} fusion(f32[16,1024]{0,1:T(8,128)S(1)} %copy.27, s32[1024]{0:T(1024)S(1)} %fusion.37), kind=kCustom, calls=%fused_computation.3.clone | custom fusion | bytes 135168 | tf_op jit(solution)/shard_map/jit(_take)/gather | solution.py:102
  149.0 10.8 %all-reduce = (f32[16]{0:T(128)S(1)}, f32[16]{0:T(128)S(1)}) all-reduce(f32[16]{0:T(128)S(1)} %get-tuple-element.62, f32[16]{0:T(128)S(1)} %get-tuple-element.61), channel_id=1, replica_groups=mesh['parts'=2,'sub'=4,'row'=2,'col'=2] {'sub'}, use_global_device_ids=true, to_apply=%region_8.10 | all-reduce | flops 32 | bytes 256 | tf_op jit(solution)/shard_map/psum | solution.py:27
  (81 shorter events, 28.8 us)
Async XLA Ops:
  0.6 34.3 %copy-start = (bf16[1,24,1024]{2,1,0:T(8,128)(2,1)S(1)}, bf16[1,24,1024]{2,1,0:T(8,128)(2,1)}, u32[]{:S(2)}) copy-start(bf16[1,24,1024]{2,1,0:T(8,128)(2,1)} %param.18) | copy-start | bytes 147460
  0.6 20.7 %copy-start.5 = (f32[1,1024]{1,0:T(1,128)S(1)}, f32[1,1024]{1,0:T(1,128)}, u32[]{:S(2)}) copy-start(f32[1,1024]{1,0:T(1,128)} %param.16) | copy-start | bytes 12292
  0.7 20.6 %copy-start.2 = (s32[1,1024]{1,0:T(1,128)S(1)}, s32[1,1024]{1,0:T(1,128)}, u32[]{:S(2)}) copy-start(s32[1,1024]{1,0:T(1,128)} %param.23) | copy-start | bytes 12292
  1.5 19.8 %collective-permute-start.1 = (bf16[16,1024]{1,0:T(8,128)(2,1)S(1)}, bf16[16,1024]{1,0:T(8,128)(2,1)S(1)}, u32[]{:S(2)}, u32[]{:S(2)}) collective-permute-start(bf16[16,1024]{1,0:T(8,128)(2,1)S(1)} %bitcast_convert_fusion), channel_id=1, source_target_pairs={{0,12},{4,0},{8,4},{12,8},{1,13},{5,1},{9,5},{13,9},{2,14},{6,2},{... | collective-permute-start | bytes 98312 | tf_op jit(solution)/shard_map/ppermute | solution.py:19
  7.3 9.4 %collective-permute-start = (bf16[1,1024]{1,0:T(2,128)(2,1)S(1)}, bf16[1,1024]{1,0:T(2,128)(2,1)S(1)}, u32[]{:S(2)}, u32[]{:S(2)}) collective-permute-start(bf16[1,1024]{1,0:T(2,128)(2,1)S(1)} %convert_element_type.71), channel_id=1, source_target_pairs={{0,12},{4,0},{8,4},{12,8},{1,13},{5,1},{9,5},{13,9},{2,14},{6,2},{... | collective-permute-start | bytes 6152 | tf_op jit(solution)/shard_map/ppermute | solution.py:19
  16.7 49.1 %copy-start.3 = (f32[48,48]{1,0:T(8,128)S(1)}, f32[48,48]{1,0:T(8,128)}, u32[]{:S(2)}) copy-start(f32[48,48]{1,0:T(8,128)} %param.19) | copy-start | bytes 27652
  21.3 53.5 %copy-start.4 = (s32[1,1024]{1,0:T(1,128)S(1)}, s32[1,1024]{1,0:T(1,128)}, u32[]{:S(2)}) copy-start(s32[1,1024]{1,0:T(1,128)} %param.22) | copy-start | bytes 12292
  24.5 58.5 %copy-start.1 = (f32[1,16,1024]{2,1,0:T(8,128)S(1)}, f32[1,16,1024]{2,1,0:T(8,128)}, u32[]{:S(2)}) copy-start(f32[1,16,1024]{2,1,0:T(8,128)} %param.15) | copy-start | bytes 196612
  70.9 5.7 %collective-permute-start.2 = (bf16[16,1024]{1,0:T(8,128)(2,1)S(1)}, bf16[16,1024]{1,0:T(8,128)(2,1)S(1)}, u32[]{:S(2)}, u32[]{:S(2)}) collective-permute-start(bf16[16,1024]{1,0:T(8,128)(2,1)S(1)} %get-tuple-element.102), channel_id=1, source_target_pairs={{0,4},{4,8},{8,12},{12,0},{1,5},{5,9},{9,13},{13,1},{2,6},{6,10},{... | collective-permute-start | bytes 98312 | tf_op jit(solution)/shard_map/ppermute | solution.py:19
  71.0 8.8 %collective-permute-start.3 = (bf16[16,1024]{1,0:T(8,128)(2,1)S(1)}, bf16[16,1024]{1,0:T(8,128)(2,1)S(1)}, u32[]{:S(2)}, u32[]{:S(2)}) collective-permute-start(bf16[16,1024]{1,0:T(8,128)(2,1)S(1)} %get-tuple-element.103), channel_id=1, source_target_pairs={{0,12},{4,0},{8,4},{12,8},{1,13},{5,1},{9,5},{13,9},{2,14},{6,2},{... | collective-permute-start | bytes 98312 | tf_op jit(solution)/shard_map/ppermute | solution.py:19
  138.6 3.9 %collective-permute-start.5 = (bf16[16,1024]{1,0:T(8,128)(2,1)S(1)}, bf16[16,1024]{1,0:T(8,128)(2,1)S(1)}, u32[]{:S(2)}, u32[]{:S(2)}) collective-permute-start(bf16[16,1024]{1,0:T(8,128)(2,1)S(1)} %get-tuple-element.100), channel_id=1, source_target_pairs={{0,12},{4,0},{8,4},{12,8},{1,13},{5,1},{9,5},{13,9},{2,14},{6,2},{... | collective-permute-start | bytes 98312 | tf_op jit(solution)/shard_map/ppermute | solution.py:19
  139.2 6.5 %collective-permute-start.4 = (bf16[16,1024]{1,0:T(8,128)(2,1)S(1)}, bf16[16,1024]{1,0:T(8,128)(2,1)S(1)}, u32[]{:S(2)}, u32[]{:S(2)}) collective-permute-start(bf16[16,1024]{1,0:T(8,128)(2,1)S(1)} %get-tuple-element.101), channel_id=1, source_target_pairs={{0,4},{4,8},{8,12},{12,0},{1,5},{5,9},{9,13},{13,1},{2,6},{6,10},{... | collective-permute-start | bytes 98312 | tf_op jit(solution)/shard_map/ppermute | solution.py:19
